TPU v7x, 32 devices: a whole 2x2x4 slice. The times are simulated.
32 devices in a mesh: replica: 8 (over z, core), shard: 4 (over y, x).
Axes of the slice: x: 2, y: 2, z: 4, core: 2. Of those that a mesh axis runs over, the one named last changes fastest.
Arguments:
- tokens: bfloat16 [32768, 2560], P(('replica', 'shard')), may hold values from -6 to 6
- w_in: bfloat16 [2560, 10496], P('shard'), may hold values from -0.125 to 0.125
- w_dt: bfloat16 [2560, 80], P('shard'), may hold values from -0.125 to 0.125
- w_out: bfloat16 [5120, 2560], P('shard'), may hold values from -0.078125 to 0.078125
- norm_gain: float32 [2560], replicated, may hold values from 0.5 to 1.5
- conv_weight: float32 [4, 5376], replicated, may hold values from -3 to 3
- conv_bias: float32 [5376], replicated, may hold values from -1.5 to 1.5
- dt_bias: float32 [80], replicated, may hold values from -5 to -1
- a_log: float32 [80], replicated, may hold values from -3 to 2.5
- d_skip: float32 [80], replicated, may hold values from 0.5 to 1.5
- gate_gain: float32 [5120], replicated, may hold values from 0.5 to 1.5
- cotangent: bfloat16 [32768, 2560], P(('replica', 'shard')), may hold values from -8 to 8
Outputs:
- result: bfloat16 [32768, 2560], P(('replica', 'shard'))
- token_grad: float32 [32768, 2560], P(('replica', 'shard'))
- grad_w_in: float32 [2560, 10496], P('shard')
- grad_w_dt: float32 [2560, 80], P('shard')
- grad_w_out: float32 [5120, 2560], P('shard')
- grad_norm_gain: float32 [2560], replicated
- grad_conv_weight: float32 [4, 5376], replicated
- grad_conv_bias: float32 [5376], replicated
- grad_dt_bias: float32 [80], replicated
- grad_a_log: float32 [80], replicated
- grad_d_skip: float32 [80], replicated
- grad_gate_gain: float32 [5120], replicated
All inputs are finite; a program needn't handle non-finite values.
Results may differ from a plain program's by a relative error of at most 0.017.
Values may be sent and summed in bfloat16 or wider, within the bound.
No kernel may reach another device: no remote copies, remote signals or barrier semaphores. Data moves between devices by JAX's collectives and lax.ppermute only.
A program may use at most 768 MiB of HBM per device.

v0:
```python
import jax
import jax.numpy as jnp
from jax import lax
from jax.sharding import PartitionSpec as P

H = 80
P_SIZE = 64
E = 5120
NST = 128
CONVK = 4
SPAN = 256
eps = 1e-05


def rms_norm(tokens_f, gain):
    return tokens_f * lax.rsqrt(jnp.mean(tokens_f * tokens_f, axis=-1, keepdims=True) + eps) * gain


def contract_rows(left, right):
    return lax.dot_general(
        left, right, (((0,), (0,)), ((), ())), preferred_element_type=jnp.float32
    )


def contract_cols(left, right):
    return lax.dot_general(
        left, right, (((1,), (1,)), ((), ())), preferred_element_type=jnp.float32
    )


def ssd_scan(values, step_size, log_decay, in_state, out_state):
    length = values.shape[0]
    blocks = length // SPAN
    highest = lax.Precision.HIGHEST
    values4 = values.reshape(blocks, SPAN, H, P_SIZE)
    decay_blk = log_decay.reshape(blocks, SPAN, H).transpose(0, 2, 1)
    step_blk = step_size.reshape(blocks, SPAN, H).transpose(0, 2, 1)
    in_blk = in_state.reshape(blocks, SPAN, NST)
    out_blk = out_state.reshape(blocks, SPAN, NST)
    running = jnp.cumsum(decay_blk, axis=2)
    gap = running[:, :, :, None] - running[:, :, None, :]
    lower = jnp.tril(jnp.ones((SPAN, SPAN), dtype=bool))
    weights = jnp.where(lower, jnp.exp(jnp.where(lower, gap, 0.0)), 0.0)
    intersection = jnp.einsum("bln,bsn->bls", out_blk, in_blk, precision=highest)
    scores = weights * intersection[:, None, :, :] * step_blk[:, :, None, :]
    inner = jnp.einsum("bhls,bshp->blhp", scores, values4, precision=highest)
    to_end = jnp.exp(running[:, :, -1:] - running) * step_blk
    local = jnp.einsum("bsn,bhs,bshp->bhpn", in_blk, to_end, values4, precision=highest)
    whole_decay = jnp.exp(running[:, :, -1])

    def carry_state(state, item):
        decay_now, add_now = item
        return (state * decay_now[:, None, None] + add_now, state)

    _, prior = lax.scan(carry_state, jnp.zeros_like(local[0]), (whole_decay, local))
    outer = jnp.einsum("bln,bhpn,bhl->blhp", out_blk, prior, jnp.exp(running), precision=highest)
    return (inner + outer).reshape(length, H, P_SIZE)


def mixer(project, dt_raw, conv_weight, conv_bias, dt_bias, a_log, d_skip, gate_gain):
    length = project.shape[0]
    gate_part = project[:, :E]
    conv_in = project[:, E:]
    padded = jnp.pad(conv_in, ((CONVK - 1, 0), (0, 0)))
    conv_out = conv_bias + padded[0:length] * conv_weight[0]
    for offset in range(1, CONVK):
        conv_out = conv_out + padded[offset : offset + length] * conv_weight[offset]
    activ = jax.nn.silu(conv_out)
    values = activ[:, :E].reshape(length, H, P_SIZE)
    in_state = activ[:, E : E + NST]
    out_state = activ[:, E + NST :]
    step_size = jax.nn.softplus(dt_raw + dt_bias)
    log_decay = -jnp.exp(a_log) * step_size
    mixed = ssd_scan(values, step_size, log_decay, in_state, out_state) + d_skip[:, None] * values
    gated = mixed.reshape(length, E) * jax.nn.silu(gate_part)
    return rms_norm(gated, gate_gain)


def body(
    tokens,
    w_in,
    w_dt,
    w_out,
    norm_gain,
    conv_weight,
    conv_bias,
    dt_bias,
    a_log,
    d_skip,
    gate_gain,
    cotangent,
):
    tokens_f = tokens.astype(jnp.float32)
    normed_f, norm_pull = jax.vjp(rms_norm, tokens_f, norm_gain)
    normed = normed_f.astype(jnp.bfloat16)
    pieces = (
        lax.all_gather(w_in, "shard", axis=0, tiled=True),
        lax.all_gather(w_dt, "shard", axis=0, tiled=True),
    )
    columns = normed
    project = jnp.dot(columns, pieces[0], preferred_element_type=jnp.float32)
    dt_raw = jnp.dot(columns, pieces[1], preferred_element_type=jnp.float32)
    gated_f, mixer_pull = jax.vjp(
        mixer, project, dt_raw, conv_weight, conv_bias, dt_bias, a_log, d_skip, gate_gain
    )
    gated = gated_f.astype(jnp.bfloat16)
    columns = gated
    mixed_out = jnp.dot(
        columns,
        lax.all_gather(w_out, "shard", axis=0, tiled=True),
        preferred_element_type=jnp.float32,
    )
    result = (tokens_f + mixed_out).astype(jnp.bfloat16)
    grad_out = lax.psum_scatter(
        contract_rows(gated, cotangent).astype(jnp.bfloat16),
        "shard",
        scatter_dimension=0,
        tiled=True,
    ).astype(jnp.float32)
    back_gated = contract_cols(cotangent, lax.all_gather(w_out, "shard", axis=0, tiled=True))
    pulled = mixer_pull(back_gated)
    back_proj = pulled[0].astype(jnp.bfloat16)
    back_dt = pulled[1].astype(jnp.bfloat16)
    grad_in, grad_dt = (
        lax.psum_scatter(
            contract_rows(normed, back_proj).astype(jnp.bfloat16),
            "shard",
            scatter_dimension=0,
            tiled=True,
        ).astype(jnp.float32),
        lax.psum_scatter(
            contract_rows(normed, back_dt).astype(jnp.bfloat16),
            "shard",
            scatter_dimension=0,
            tiled=True,
        ).astype(jnp.float32),
    )
    grad_in, grad_dt, grad_out = (
        lax.psum(grad_in.astype(jnp.bfloat16), "replica").astype(jnp.float32),
        lax.psum(grad_dt.astype(jnp.bfloat16), "replica").astype(jnp.float32),
        lax.psum(grad_out.astype(jnp.bfloat16), "replica").astype(jnp.float32),
    )
    pieces = (
        lax.all_gather(w_in, "shard", axis=0, tiled=True),
        lax.all_gather(w_dt, "shard", axis=0, tiled=True),
    )
    part_cols = contract_cols(back_proj, pieces[0]) + contract_cols(back_dt, pieces[1])
    back_tokens, grad_norm = norm_pull(part_cols)
    token_grad = cotangent.astype(jnp.float32) + back_tokens
    small_grads = lax.psum(
        (grad_norm, pulled[2], pulled[3], pulled[4], pulled[5], pulled[6], pulled[7]),
        ("replica", "shard"),
    )
    return (
        result,
        token_grad,
        grad_in,
        grad_dt,
        grad_out,
        small_grads[0],
        small_grads[1],
        small_grads[2],
        small_grads[3],
        small_grads[4],
        small_grads[5],
        small_grads[6],
    )


def solution(mesh):
    placed = (
        P(("replica", "shard"), None),
        P("shard", None),
        P("shard", None),
        P("shard", None),
        P(),
        P(),
        P(),
        P(),
        P(),
        P(),
        P(),
        P(("replica", "shard"), None),
    )
    return jax.shard_map(
        body,
        mesh=mesh,
        in_specs=placed,
        out_specs=(
            P(("replica", "shard"), None),
            P(("replica", "shard"), None),
            P("shard", None),
            P("shard", None),
            P("shard", None),
            P(),
            P(),
            P(),
            P(),
            P(),
            P(),
            P(),
        ),
        check_vma=False,
    )
```

profile of v0, /device:TPU:8, one launch (start us, length us, event | category | flops | bytes accessed | tf_op | source)
XLA Modules:
  0.0 2894.5 jit_solution(18246477915600876768)
XLA Ops:
  38.6 438.9 %all-gather.3.cloned.1.call-done = bf16[2560,10496]{1,0:T(8,128)(2,1)} async-done(((bf16[640,10496]{1,0:T(8,128)(2,1)}), bf16[2560,10496]{1,0:T(8,128)(2,1)}) %all-gather.3.cloned.1.call-update) | async-done | bytes 53739536 | tf_op jit(solution)/shard_map/all_gather | solution.py:97
  477.4 65.4 %fusion.87 = f32[1024,10496]{1,0:T(8,128)} fusion(bf16[2560,10496]{1,0:T(8,128)(2,1)} %all-gather.3.cloned.1.call-done, bf16[1024,2560]{1,0:T(8,128)(2,1)} %param.16, f32[2560]{0:T(1024)S(1)} %copy-done.54, f32[1024]{0:T(1024)S(1)} %fusion.78), kind=kOutput, calls=%fused_computation.169 | convolution fusion | flops 55039754240 | bytes 101988352 | tf_op jit(solution)/shard_map/dot_general | solution.py:101
  558.9 48.1 %fusion.26 = (f32[1024,5376]{1,0:T(8,128)}, f32[1024,5376]{1,0:T(8,128)}) fusion(f32[1024,5376]{1,0:T(8,128)} %slice.71, f32[5376]{0:T(1024)S(1)} %get-tuple-element.251, f32[5376]{0:T(1024)S(1)} %get-tuple-element.252, f32[5376]{0:T(1024)S(1)} %get-tuple-element.250, f32[5376]{0:T(1024)S(1)} %get-tuple-element.249, f32[5376]{0:T(1024)S(1)} %copy-done.62), kind=kLoop, calls=%fused_computation.51 | loop fusion | flops 66060288 | bytes 66167808 | tf_op jit(solution)/shard_map/jvp(jit(silu))/mul | solution.py:68
  773.9 103.0 %fusion.33 = f32[4,256,80,64]{1,3,2,0:T(8,128)} fusion(f32[4,80,64,256]{3,2,1,0:T(8,128)S(1)} %fusion.96, f32[4,256,80]{1,2,0:T(8,128)S(1)} %copy-done.12, f32[4,80,256]{2,1,0:T(8,128)S(1)} %bitcast.216, f32[4,256,256]{2,1,0:T(8,128)S(1)} %copy-done.23, f32[4,80,256]{2,1,0:T(8,128)S(1)} %copy-done.26, pred[256,256]{1,0:T(8,128)(4,1)S(1)} %copy-done.52, ...), kind=kOutput, calls=%fused_computation.61 | convolution fusion | flops 16221470720 | bytes 65011712 | tf_op jit(solution)/shard_map/jvp(bhls,bshp->blhp)/dot_general | solution.py:46
  973.0 37.9 %multiply_reduce_fusion.8 = (f32[5120]{0:T(1024)}, f32[1024]{0:T(1024)S(1)}, f32[1024,5120]{1,0:T(8,128)}) fusion(f32[1024,5120]{1,0:T(8,128)} %get-tuple-element.294, f32[1024]{0:T(1024)S(1)} %fusion.79, f32[5120]{0:T(1024)S(1)} %copy-done.63, bf16[1024,2560]{1,0:T(8,128)(2,1)} %param.27, bf16[5120,2560]{1,0:T(8,128)(2,1)} %all-gather.5.cloned.1.call-done), kind=kOutput, calls=%fused_computation.68 | convolution fusion | flops 26874998784 | bytes 73449472 | tf_op jit(solution)/shard_map/dot_general | solution.py:26
  1010.9 50.2 %multiply_reduce_fusion.9 = (f32[5120]{0:T(1024)}, f32[1024,5120]{1,0:T(8,128)}, f32[1024,5120]{1,0:T(8,128)}) fusion(f32[1024,5376]{1,0:T(8,128)} %get-tuple-element.295, f32[1024,10496]{1,0:T(8,128)} %fusion.87, f32[1024,5120]{1,0:T(8,128)} %get-tuple-element.294, f32[1024]{0:T(1024)S(1)} %multiply_multiply_fusion.2, f32[1024]{0:T(1024)S(1)} %fusion.79, ...), kind=kLoop, calls=%fused_computation.69 | loop fusion | flops 110095360 | bytes 146870272 | tf_op jit(solution)/shard_map/transpose(jvp())/reduce_sum | solution.py:74
  1135.7 136.2 %fusion.11 = (f32[4,80,256]{2,1,0:T(8,128)}, f32[4,80,256]{2,1,0:T(8,128)}, f32[4,80,256]{2,1,0:T(8,128)}, f32[4,256,256]{2,1,0:T(8,128)}) fusion(f32[4,80,256]{2,1,0:T(8,128)S(1)} %bitcast.217, f32[4,256,256]{2,1,0:T(8,128)S(1)} %copy-done.24, f32[4,80,256]{2,1,0:T(8,128)S(1)} %copy-done.27, pred[256,256]{1,0:T(8,128)(4,1)S(1)} %copy-done.53, ...), kind=kOutput, calls=%fused_computation.23 | convolution fusion | flops 16420192256 | bytes 45744128 | tf_op jit(solution)/shard_map/transpose(jvp(bhls,bshp->blhp))/dot_general | solution.py:46
  1271.9 76.8 %fusion.6 = f32[4,80,64,256]{3,2,1,0:T(8,128)} fusion(f32[4,80,256]{2,1,0:T(8,128)S(1)} %bitcast.218, f32[4,256,256]{2,1,0:T(8,128)S(1)} %copy-done.24, f32[4,80,256]{2,1,0:T(8,128)S(1)} %copy-done.27, pred[256,256]{1,0:T(8,128)(4,1)S(1)} %copy-done.53, f32[4,80,64,256]{3,0,2,1:T(4,128)S(1)} %bitcast.191), kind=kOutput, calls=%fused_computation.19 | convolution fusion | flops 16210984960 | bytes 43712512 | tf_op jit(solution)/shard_map/transpose(jvp(bhls,bshp->blhp))/dot_general | solution.py:46
  1385.2 36.5 %while.35 = (s32[]{:T(128)}, f32[80,64,128]{2,1,0:T(8,128)}, f32[4,80]{1,0:T(4,128)S(1)}, f32[4,80,64,128]{3,1,2,0:T(8,128)}, f32[4,80,64,128]{3,2,1,0:T(8,128)}...) while((s32[]{:T(128)}, f32[80,64,128]{2,1,0:T(8,128)}, ...), condition=%wide.region_10.11_spmd.clone, body=%wide.region_8.10_spmd.clone.sunk | while | flops 3276724 | bytes 18352148 | solution.py:55
  1421.9 34.9 %bitcast_add_fusion.2 = (f32[4,256,80,64]{1,2,3,0:T(8,128)}, f32[4,256,80,64]{1,2,3,0:T(8,128)}) fusion(f32[4,80,64,256]{3,2,1,0:T(8,128)} %fusion.6, f32[4,256,80]{1,2,0:T(8,128)S(1)} %copy-done.19, f32[4,256,128,1]{2,1,3,0:T(8,128)S(1)} %bitcast.204, f32[4,80,64,128]{3,1,2,0:T(8,128)} %get-tuple-element.189), kind=kOutput, calls=%fused_computation.55 | convolution fusion | flops 8063549440 | bytes 74252288 | tf_op jit(solution)/shard_map/transpose(jvp(bsn,bhs,bshp->bhpn))/dot_general | solution.py:48
  1500.6 35.7 %convolution_convert_fusion.1 = bf16[5120,2560]{1,0:T(8,128)(2,1)} fusion(bf16[1024,2560]{1,0:T(8,128)(2,1)} %param.27, f32[1024,5120]{1,0:T(8,128)} %get-tuple-element.294, f32[5120]{0:T(1024)S(1)} %copy-done.64, f32[1024]{0:T(1024)S(1)} %copy-done.68), kind=kOutput, calls=%fused_computation.40 | convolution fusion | flops 26872381440 | bytes 52453376 | tf_op jit(solution)/shard_map/dot_general | solution.py:20
  1536.3 36.8 %copy.190 = f32[4,256,80,64]{3,2,1,0:T(8,128)} copy(f32[4,256,80,64]{1,2,3,0:T(8,128)} %get-tuple-element.316) | data formatting | bytes 41943040 | tf_op jit(solution)/shard_map/transpose(jvp())/reshape | solution.py:35
  1606.3 40.5 %fusion.59 = f32[4,256,128]{2,1,0:T(8,128)S(1)} fusion(f32[4,80,64,128]{3,2,1,0:T(8,128)} %get-tuple-element.486, f32[4,256,80,64]{1,0,3,2:T(4,128)} %reshape.225, f32[4,256,80]{1,2,0:T(8,128)S(1)} %copy-done.14), kind=kOutput, calls=%fused_computation.111 | convolution fusion | flops 8058306560 | bytes 32309248 | tf_op jit(solution)/shard_map/transpose(jvp(bln,bhpn,bhl->blhp))/dot_general | solution.py:56
  1647.9 37.0 %convolution_bitcast_fusion = f32[4,256,128]{2,1,0:T(8,128)S(1)} fusion(f32[4,256,80,64]{1,2,3,0:T(8,128)} %copy-done.2, f32[4,80,64,128]{3,1,2,0:T(8,128)} %get-tuple-element.189), kind=kOutput, calls=%fused_computation.112 | convolution fusion | flops 8053063680 | bytes 31981568 | tf_op jit(solution)/shard_map/transpose(jvp(bsn,bhs,bshp->bhpn))/dot_general | solution.py:48
  1704.7 56.3 %multiply_reduce_fusion.4 = (f32[5376]{0:T(1024)S(1)}, f32[5376]{0:T(1024)S(1)}, f32[5376]{0:T(1024)S(1)}, f32[5376]{0:T(1024)}, f32[5376]{0:T(1024)S(1)}, /*index=5*/f32[1024,5376]{1,0:T(8,128)}) fusion(f32[1024,5376]{1,0:T(8,128)} %slice.71, f32[1024,10496]{1,0:T(8,128)} %fusion.87, f32[1024,5376]{1,0:T(8,128)} %get-tuple-element.296, ...), kind=kLoop, calls=%fused_computation.48 | loop fusion | flops 110073600 | bytes 110208000 | tf_op jit(solution)/shard_map/transpose(jvp())/reduce_sum | solution.py:67
  1760.9 34.7 %broadcast_multiply_fusion = (f32[1024,5376]{1,0:T(8,128)}, f32[1024,5376]{1,0:T(8,128)}, f32[1024,5376]{1,0:T(8,128)}, f32[1024,5376]{1,0:T(8,128)}) fusion(f32[1024,5376]{1,0:T(8,128)} %get-tuple-element.292, f32[5376]{0:T(1024)S(1)} %copy-done.41, f32[5376]{0:T(1024)S(1)} %copy-done.37, f32[5376]{0:T(1024)S(1)} %copy-done.39, f32[5376]{0:T(1024)S(1)} %copy-done.43), kind=kLoop, calls=%fused_computation.92 | loop fusion | flops 22020096 | bytes 110186496 | tf_op jit(solution)/shard_map/transpose(jvp())/mul | solution.py:67
  1795.6 36.1 %pad_add_fusion = f32[1024,5376]{1,0:T(8,128)} fusion(f32[1024,5376]{1,0:T(8,128)} %get-tuple-element.302, f32[1024,5376]{1,0:T(8,128)} %get-tuple-element.303, f32[1024,5376]{1,0:T(8,128)} %get-tuple-element.304, f32[1024,5376]{1,0:T(8,128)} %get-tuple-element.301), kind=kLoop, calls=%fused_computation.43 | loop fusion | flops 16515072 | bytes 110100480 | tf_op jit(solution)/shard_map/transpose(jvp())/add_any | solution.py:65
  1831.7 71.6 %convolution_convert_fusion = bf16[2560,10496]{1,0:T(8,128)(2,1)} fusion(f32[1024,5120]{1,0:T(8,128)} %get-tuple-element.300, f32[1024,5376]{1,0:T(8,128)} %pad_add_fusion, bf16[1024,2560]{1,0:T(8,128)(2,1)} %param.16, f32[2560]{0:T(1024)S(1)} %copy-done.56, f32[1024]{0:T(1024)S(1)} %copy-done.61), kind=kOutput, calls=%fused_computation.21 | convolution fusion | flops 55088119808 | bytes 101988352 | tf_op jit(solution)/shard_map/dot_general | solution.py:20
  1905.3 450.1 %reduce-scatter.6.cloned.1.call-done = bf16[640,10496]{1,0:T(8,128)(2,1)} async-done(((bf16[2560,10496]{1,0:T(8,128)(2,1)}), bf16[640,10496]{1,0:T(8,128)(2,1)}) %reduce-scatter.6.cloned.1.call-update) | async-done | bytes 13434896 | tf_op jit(solution)/shard_map/reduce_scatter | solution.py:125
  2355.5 72.5 %fusion.58 = f32[1024,2560]{1,0:T(8,128)} fusion(bf16[2560,10496]{1,0:T(8,128)(2,1)} %all-gather.3.cloned.1.call-done, f32[1024,5120]{1,0:T(8,128)} %get-tuple-element.300, f32[1024,5376]{1,0:T(8,128)} %pad_add_fusion), kind=kOutput, calls=%fused_computation.108 | convolution fusion | flops 55050764288 | bytes 107216896 | tf_op jit(solution)/shard_map/dot_general | solution.py:26
  2452.0 38.7 %fusion.48 = bf16[1024,2560]{1,0:T(8,128)(2,1)} fusion(bf16[1024,2560]{1,0:T(8,128)(2,1)S(1)} %bitcast.197, bf16[5120,2560]{1,0:T(8,128)(2,1)} %all-gather.5.cloned.1.call-done, f32[1024,5120]{1,0:T(8,128)} %get-tuple-element.294, f32[5120]{0:T(1024)S(1)} %copy-done.65, f32[1024]{0:T(1024)S(1)} %copy-done.69), kind=kOutput, calls=%fused_computation.100 | convolution fusion | flops 26867138560 | bytes 57696256 | tf_op jit(solution)/shard_map/dot_general | solution.py:108
  2491.0 42.3 %all-reduce.16 = (f32[2560]{0:T(1024)}, f32[5376]{0:T(1024)}, f32[80]{0:T(128)}, f32[80]{0:T(128)}, f32[80]{0:T(128)}, /*index=5*/f32[5120]{0:T(1024)}) all-reduce(f32[2560]{0:T(1024)S(1)} %get-tuple-element.247, f32[5376]{0:T(1024)S(1)} %copy-done.47, ...), channel_id=1, replica_groups=mesh['replica'=8,'shard'=4] {'replica','shard'}, use_global_device_ids=true, to_apply=%region_25.26 | all-reduce | flops 13296 | bytes 106368 | tf_op jit(solution)/shard_map/psum | solution.py:150
  2533.3 224.0 %all-reduce.23.cloned.1.call-done = (bf16[640,10496]{1,0:T(8,128)(2,1)}, bf16[640,80]{0,1:T(8,128)(2,1)}, bf16[1280,2560]{1,0:T(8,128)(2,1)}) async-done(((bf16[640,10496]{1,0:T(8,128)(2,1)}, bf16[640,80]{0,1:T(8,128)(2,1)}, bf16[1280,2560]{1,0:T(8,128)(2,1)}), (bf16[640,10496]{1,0:T(8,128)(2,1)}, bf16[640,80]{0,1:T(8,128)(2,1)}, bf16[1280,2560]{1,0:T(8,128)(2,1)})) %all-reduce.23.cloned.1.call-update) | async-done | bytes 20090896 | tf_op jit(solution)/shard_map/psum | solution.py:139
  2778.5 107.4 %all-reduce.21.cloned.1.call-done = f32[4,5376]{1,0:T(4,128)} async-done(((f32[4,5376]{1,0:T(4,128)}), f32[4,5376]{1,0:T(4,128)}) %all-reduce.21.cloned.1.call-update) | async-done | bytes 86032 | tf_op jit(solution)/shard_map/psum | solution.py:150
  (305 shorter events, 621.6 us)
Async XLA Ops:
  7.2 470.2 %all-gather.3.cloned.1.call-start = ((), (), s32[]{:S(2)}) async-start(), calls=%async_computation.3 | async-start | bytes 67174400 | tf_op jit(solution)/shard_map/all_gather | solution.py:97
  8.0 965.0 %all-gather.5.cloned.1.call-start = ((), (), s32[]{:S(2)}) async-start(), calls=%async_computation.4 | async-start | bytes 32768000 | tf_op jit(solution)/shard_map/all_gather | solution.py:110
  8.7 1894.8 %reduce-scatter.10.cloned.1.call-start = ((), (), s32[]{:S(2)}) async-start(), calls=%async_computation.8 | async-start | bytes 819200
  13.0 529.8 %copy-start.59 = (f32[1024]{0:T(1024)}, f32[1024]{0:T(1024)S(1)}, u32[]{:S(2)}) copy-start(f32[1024]{0:T(1024)S(1)} %fusion.78) | copy-start | bytes 12292
  13.3 545.6 %copy-start.36 = (f32[5376]{0:T(1024)}, f32[5376]{0:T(1024)S(1)}, u32[]{:S(2)}) copy-start(f32[5376]{0:T(1024)S(1)} %get-tuple-element.249) | copy-start | bytes 64516
  13.3 545.6 %copy-start.38 = (f32[5376]{0:T(1024)}, f32[5376]{0:T(1024)S(1)}, u32[]{:S(2)}) copy-start(f32[5376]{0:T(1024)S(1)} %get-tuple-element.250) | copy-start | bytes 64516
  13.3 545.6 %copy-start.40 = (f32[5376]{0:T(1024)}, f32[5376]{0:T(1024)S(1)}, u32[]{:S(2)}) copy-start(f32[5376]{0:T(1024)S(1)} %get-tuple-element.251) | copy-start | bytes 64516
  13.3 545.6 %copy-start.42 = (f32[5376]{0:T(1024)}, f32[5376]{0:T(1024)S(1)}, u32[]{:S(2)}) copy-start(f32[5376]{0:T(1024)S(1)} %get-tuple-element.252) | copy-start | bytes 64516
  30.6 512.3 %copy-start.15 = (f32[1024,80]{0,1:T(8,128)}, f32[1024,80]{0,1:T(8,128)S(1)}, u32[]{:S(2)}) copy-start(f32[1024,80]{0,1:T(8,128)S(1)} %get-tuple-element.312) | copy-start | bytes 983044
  33.3 509.6 %copy-start.10 = (f32[4,80,2,128]{3,1,2,0:T(8,128)}, f32[4,80,2,128]{3,1,2,0:T(8,128)S(1)}, u32[]{:S(2)}) copy-start(f32[4,80,2,128]{3,1,2,0:T(8,128)S(1)} %reduce-window.14) | copy-start | bytes 983044
  33.6 509.2 %copy-start.44 = (f32[4,80,2]{1,2,0:T(2,128)}, f32[4,80,2]{1,2,0:T(2,128)S(1)}, u32[]{:S(2)}) copy-start(f32[4,80,2]{1,2,0:T(2,128)S(1)} %copy.144) | copy-start | bytes 7684
  34.8 508.1 %copy-start.50 = (f32[4,80]{1,0:T(4,128)}, f32[4,80]{1,0:T(4,128)S(1)}, u32[]{:S(2)}) copy-start(f32[4,80]{1,0:T(4,128)S(1)} %slice_reduce_fusion) | copy-start | bytes 3844
  671.6 74.1 %copy-start.5 = (f32[1024,128]{1,0:T(8,128)}, f32[1024,128]{1,0:T(8,128)S(1)}, u32[]{:S(2)}) copy-start(f32[1024,128]{1,0:T(8,128)S(1)} %get-tuple-element.305) | copy-start | bytes 1572868
  1500.5 404.7 %reduce-scatter.8.cloned.1.call-start = ((), (), s32[]{:S(2)}) async-start(), calls=%async_computation.6 | async-start | bytes 32768000 | tf_op jit(solution)/shard_map/reduce_scatter | solution.py:114
  1536.3 819.1 %reduce-scatter.6.cloned.1.call-start = ((), (), s32[]{:S(2)}) async-start(), calls=%async_computation.5 | async-start | bytes 67174400 | tf_op jit(solution)/shard_map/reduce_scatter | solution.py:125
  1606.3 80.5 %slice-start = ((s8[20971520]{0:T(1024)(128)(4,1)}), s8[4194304]{0:T(1024)(128)(4,1)S(1)}, s32[]{:S(2)}) async-start(s8[20971520]{0:T(1024)(128)(4,1)} %bitcast.192), calls=%async_computation.10 | async-start | bytes 8388608
  1606.3 80.5 %slice-start.1 = ((s8[20971520]{0:T(1024)(128)(4,1)}), s8[4194304]{0:T(1024)(128)(4,1)S(1)}, s32[]{:S(2)}) async-start(s8[20971520]{0:T(1024)(128)(4,1)} %bitcast.192), calls=%async_computation.11 | async-start | bytes 8388608
  1606.3 80.5 %slice-start.2 = ((s8[20971520]{0:T(1024)(128)(4,1)}), s8[4194304]{0:T(1024)(128)(4,1)S(1)}, s32[]{:S(2)}) async-start(s8[20971520]{0:T(1024)(128)(4,1)} %bitcast.192), calls=%async_computation.12 | async-start | bytes 8388608
  1606.3 80.5 %slice-start.3 = ((s8[20971520]{0:T(1024)(128)(4,1)}), s8[4194304]{0:T(1024)(128)(4,1)S(1)}, s32[]{:S(2)}) async-start(s8[20971520]{0:T(1024)(128)(4,1)} %bitcast.192), calls=%async_computation.13 | async-start | bytes 8388608
  1704.6 56.3 %copy-start.43 = (f32[5376]{0:T(1024)S(1)}, f32[5376]{0:T(1024)}, u32[]{:S(2)}) copy-start(f32[5376]{0:T(1024)} %copy-done.42) | copy-start | bytes 64516
  1903.4 853.9 %all-reduce.23.cloned.1.call-start = ((), (), s32[]{:S(2)}) async-start(), calls=%async_computation.9 | async-start | bytes 40181760 | tf_op jit(solution)/shard_map/psum | solution.py:139
  2355.4 72.6 %copy-start.21 = (bf16[2560,80]{0,1:T(8,128)(2,1)S(1)}, bf16[2560,80]{0,1:T(8,128)(2,1)}, u32[]{:S(2)}) copy-start(bf16[2560,80]{0,1:T(8,128)(2,1)} %copy-done.20) | copy-start | bytes 1228804
  2355.4 72.6 %copy-start.29 = (bf16[1024,80]{0,1:T(8,128)(2,1)S(1)}, bf16[1024,80]{0,1:T(8,128)(2,1)}, u32[]{:S(2)}) copy-start(bf16[1024,80]{0,1:T(8,128)(2,1)} %copy-done.28) | copy-start | bytes 491524
  2355.4 530.4 %all-reduce.21.cloned.1.call-start = ((), (), s32[]{:S(2)}) async-start(), calls=%async_computation.7 | async-start | bytes 172032 | tf_op jit(solution)/shard_map/psum | solution.py:150
  (68 other events, 1916.6 us)
Sparse Core Ops, SparseCore 0:
  9.9 467.4 all-gather.2
  479.3 236.3 all-gather.4
  1500.7 25.7 reduce-scatter.9
  1536.4 230.6 reduce-scatter.7
  1903.5 451.8 reduce-scatter.5
  2358.9 398.3 all-reduce.22
  2763.5 122.3 all-reduce.20
where the time goes:
time: 2900 us; the launch traced here: 2890 us
  waiting for transfers between devices  1220 us (42%)
  matrix products  853 us (29%)
  other arithmetic  441 us (15%)
  local copies, waits for them, and re-layouts  311 us (11%)
  blocking collectives  52.3 us (2%)
    reduce_scatter x1, waiting for transfers between devices, body(): lax.psum_scatter(contract_rows(normed, back_proj).astype(jnp.bfloat16), '...  450 us
    all_gather x1, waiting for transfers between devices, body(): lax.all_gather(w_in, 'shard', axis=0, tiled=True)  439 us
    dot_general x3, matrix products, ssd_scan(): inner = jnp.einsum('bhls,bshp->blhp', scores, values4, precision=highest)  316 us
    psum x1, waiting for transfers between devices, body(): lax.psum(grad_in.astype(jnp.bfloat16), 'replica').astype(jnp.float32)  224 us
    dot_general x3, matrix products, contract_cols(): lax.dot_general(left, right, (((1,), (1,)), ((), ())), preferred_element_...  120 us
    dot_general x3, matrix products, contract_rows(): lax.dot_general(left, right, (((0,), (0,)), ((), ())), preferred_element_...  111 us
    psum x1, waiting for transfers between devices, body(): lax.psum((grad_norm, pulled[2], pulled[3], pulled[4], pulled[5], pulled[6...  107 us
    dot_general x3, matrix products, ssd_scan(): jnp.einsum('bsn,bhs,bshp->bhpn', in_blk, to_end, values4, precision=highest)  99.6 us
  transfers between devices with their start and end apart: 7, of which 4 were waited for; matrix products, arithmetic and copies ran while one was open for 37% of the time, Pallas kernels for 0%

commit v1 on v0

--- a/solution.py
+++ b/solution.py
@@ -10,6 +10,27 @@
 CONVK = 4
 SPAN = 256
 eps = 1e-05
+
+
+def ring_gather(shard, axis, dim):
+    length, place, extent = (lax.axis_size(axis), lax.axis_index(axis), shard.shape[dim])
+    right = [(i, (i + 1) % length) for i in range(length)]
+    left = [(i, (i - 1) % length) for i in range(length)]
+    out = jnp.zeros((*shard.shape[:dim], length * extent, *shard.shape[dim + 1 :]), shard.dtype)
+    out = lax.dynamic_update_slice_in_dim(out, shard, place * extent, axis=dim)
+    from_left = from_right = shard
+    half = length // 2
+    for step in range(1, half + 1):
+        from_left = lax.ppermute(from_left, axis, right)
+        out = lax.dynamic_update_slice_in_dim(
+            out, from_left, (place - step) % length * extent, axis=dim
+        )
+        if step < length - half:
+            from_right = lax.ppermute(from_right, axis, left)
+            out = lax.dynamic_update_slice_in_dim(
+                out, from_right, (place + step) % length * extent, axis=dim
+            )
+    return out
 
 
 def rms_norm(tokens_f, gain):
@@ -93,10 +114,7 @@
     tokens_f = tokens.astype(jnp.float32)
     normed_f, norm_pull = jax.vjp(rms_norm, tokens_f, norm_gain)
     normed = normed_f.astype(jnp.bfloat16)
-    pieces = (
-        lax.all_gather(w_in, "shard", axis=0, tiled=True),
-        lax.all_gather(w_dt, "shard", axis=0, tiled=True),
-    )
+    pieces = (ring_gather(w_in, "shard", 0), lax.all_gather(w_dt, "shard", axis=0, tiled=True))
     columns = normed
     project = jnp.dot(columns, pieces[0], preferred_element_type=jnp.float32)
     dt_raw = jnp.dot(columns, pieces[1], preferred_element_type=jnp.float32)

time: 2900 us -> 4050 us (1.40)
  blocking collectives: 52.3 us -> 830 us
  waiting for transfers between devices: 1220 us -> 1540 us
  local copies, waits for them, and re-layouts: 311 us -> 376 us
    all_gather x1, blocking collectives: 9.92 us -> 789 us  [body(): lax.all_gather(w_dt, 'shard', axis=0, tiled=True)]
    ppermute x0 -> x3, waiting for transfers between devices: none -> 290 us  [the longest x2 290 us: ring_gather(): from_left = lax.ppermute(from_left, axis, right)]
    psum x1, waiting for transfers between devices: 224 us -> 273 us  [body(): lax.psum(grad_in.astype(jnp.bfloat16), 'replica').astype(jnp.float32)]
    dynamic_update_slice x0 -> x4, local copies, waits for them, and re-layouts: none -> 43.4 us  [the longest x2 24.6 us: ring_gather(): lax.dynamic_update_slice_in_dim(out, from_left, (place - step) % length *...]
  transfers between devices with their start and end apart: 7 -> 10, of which waited for: 4 -> 5; matrix products, arithmetic and copies ran while one was open for 37% -> 28% of each run, Pallas kernels for 0% -> 0%
where the time goes in v1:
time: 4050 us; the launch traced here: 4040 us
  waiting for transfers between devices  1540 us (38%)
  matrix products  849 us (21%)
  blocking collectives  830 us (20%)
  other arithmetic  423 us (10%)
  local copies, waits for them, and re-layouts  376 us (9%)
    all_gather x1, blocking collectives, body(): lax.all_gather(w_dt, 'shard', axis=0, tiled=True)  789 us
    reduce_scatter x1, waiting for transfers between devices, body(): lax.psum_scatter(contract_rows(normed, back_proj).astype(jnp.bfloat16), '...  450 us
    all_gather x1, waiting for transfers between devices, body(): lax.all_gather(w_in, 'shard', axis=0, tiled=True)  425 us
    dot_general x3, matrix products, ssd_scan(): inner = jnp.einsum('bhls,bshp->blhp', scores, values4, precision=highest)  316 us
    ppermute x2, waiting for transfers between devices, ring_gather(): from_left = lax.ppermute(from_left, axis, right)  290 us
    psum x1, waiting for transfers between devices, body(): lax.psum(grad_in.astype(jnp.bfloat16), 'replica').astype(jnp.float32)  273 us
    dot_general x3, matrix products, contract_cols(): lax.dot_general(left, right, (((1,), (1,)), ((), ())), preferred_element_...  118 us
    dot_general x3, matrix products, contract_rows(): lax.dot_general(left, right, (((0,), (0,)), ((), ())), preferred_element_...  112 us
  transfers between devices with their start and end apart: 10, of which 5 were waited for; matrix products, arithmetic and copies ran while one was open for 28% of the time, Pallas kernels for 0%

profile of v1, /device:TPU:8, one launch (start us, length us, event | category | flops | bytes accessed | tf_op | source)
XLA Modules:
  0.0 4041.1 jit_solution(13452432687074736653)
XLA Ops:
  10.2 289.8 %collective-permute-done = bf16[640,10496]{1,0:T(8,128)(2,1)} collective-permute-done((bf16[640,10496]{1,0:T(8,128)(2,1)}, bf16[640,10496]{1,0:T(8,128)(2,1)}, u32[]{:S(2)}, u32[]{:S(2)}) %collective-permute-start) | collective-permute-done | bytes 13434912 | tf_op jit(solution)/shard_map/ppermute | solution.py:24
  300.8 788.8 %all_gather.11 = bf16[2560,80]{0,1:T(8,128)(2,1)S(1)} all-gather(bf16[640,80]{0,1:T(8,128)(2,1)} %param.18), channel_id=1, replica_groups=mesh['replica'=8,'shard'=4] {'shard'}, dimensions={0}, use_global_device_ids=true | all-gather | bytes 512000 | tf_op jit(solution)/shard_map/all_gather | solution.py:117
  1171.4 63.9 %fusion.87 = f32[1024,10496]{1,0:T(8,128)} fusion(bf16[2560,10496]{1,0:T(8,128)(2,1)} %constant_dynamic-update-slice_fusion.1, bf16[1024,2560]{1,0:T(8,128)(2,1)S(1)} %bitcast.199, f32[2560]{0:T(1024)S(1)} %copy-done.58, f32[1024]{0:T(1024)S(1)} %fusion.78), kind=kOutput, calls=%fused_computation.173 | convolution fusion | flops 55039754240 | bytes 101988352 | tf_op jit(solution)/shard_map/dot_general | solution.py:119
  1251.4 44.3 %fusion.26 = (f32[1024,5376]{1,0:T(8,128)}, f32[1024,5376]{1,0:T(8,128)}) fusion(f32[1024,5376]{1,0:T(8,128)} %slice.71, f32[5376]{0:T(1024)S(1)} %copy-done.44, f32[5376]{0:T(1024)S(1)} %copy-done.46, f32[5376]{0:T(1024)S(1)} %copy-done.42, f32[5376]{0:T(1024)S(1)} %copy-done.40, f32[5376]{0:T(1024)S(1)} %copy-done.68), kind=kLoop, calls=%fused_computation.51 | loop fusion | flops 66060288 | bytes 66167808 | tf_op jit(solution)/shard_map/jvp(jit(silu))/mul | solution.py:89
  1462.2 103.0 %fusion.33 = f32[4,256,80,64]{1,3,2,0:T(8,128)} fusion(f32[4,80,64,256]{3,2,1,0:T(8,128)S(1)} %fusion.96, f32[4,256,80]{1,2,0:T(8,128)S(1)} %copy-done.14, f32[4,80,256]{2,1,0:T(8,128)S(1)} %bitcast.220, f32[4,256,256]{2,1,0:T(8,128)S(1)} %copy-done.25, f32[4,80,256]{2,1,0:T(8,128)S(1)} %copy-done.28, pred[256,256]{1,0:T(8,128)(4,1)S(1)} %copy-done.56, ...), kind=kOutput, calls=%fused_computation.61 | convolution fusion | flops 16221470720 | bytes 65011712 | tf_op jit(solution)/shard_map/jvp(bhls,bshp->blhp)/dot_general | solution.py:67
  1661.6 37.8 multiply_reduce_fusion.8
  1699.5 50.3 %multiply_reduce_fusion.9 = (f32[5120]{0:T(1024)}, f32[1024,5120]{1,0:T(8,128)}, f32[1024,5120]{1,0:T(8,128)}) fusion(f32[1024,5376]{1,0:T(8,128)} %get-tuple-element.295, f32[1024,10496]{1,0:T(8,128)} %fusion.87, f32[1024,5120]{1,0:T(8,128)} %get-tuple-element.294, f32[1024]{0:T(1024)S(1)} %multiply_multiply_fusion.2, f32[1024]{0:T(1024)S(1)} %fusion.79, ...), kind=kLoop, calls=%fused_computation.69 | loop fusion | flops 110095360 | bytes 146870272 | tf_op jit(solution)/shard_map/transpose(jvp())/reduce_sum | solution.py:95
  1823.8 136.4 %fusion.11 = (f32[4,80,256]{2,1,0:T(8,128)}, f32[4,80,256]{2,1,0:T(8,128)}, f32[4,80,256]{2,1,0:T(8,128)}, f32[4,256,256]{2,1,0:T(8,128)}) fusion(f32[4,80,256]{2,1,0:T(8,128)S(1)} %bitcast.221, f32[4,256,256]{2,1,0:T(8,128)S(1)} %copy-done.26, f32[4,80,256]{2,1,0:T(8,128)S(1)} %copy-done.29, pred[256,256]{1,0:T(8,128)(4,1)S(1)} %copy-done.57, ...), kind=kOutput, calls=%fused_computation.23 | convolution fusion | flops 16420192256 | bytes 45744128 | tf_op jit(solution)/shard_map/transpose(jvp(bhls,bshp->blhp))/dot_general | solution.py:67
  1960.2 76.8 %fusion.6 = f32[4,80,64,256]{3,2,1,0:T(8,128)} fusion(f32[4,80,256]{2,1,0:T(8,128)S(1)} %bitcast.222, f32[4,256,256]{2,1,0:T(8,128)S(1)} %copy-done.26, f32[4,80,256]{2,1,0:T(8,128)S(1)} %copy-done.29, pred[256,256]{1,0:T(8,128)(4,1)S(1)} %copy-done.57, f32[4,80,64,256]{3,0,2,1:T(4,128)S(1)} %bitcast.191), kind=kOutput, calls=%fused_computation.19 | convolution fusion | flops 16210984960 | bytes 43712512 | tf_op jit(solution)/shard_map/transpose(jvp(bhls,bshp->blhp))/dot_general | solution.py:67
  2070.7 34.9 bitcast_add_fusion.2
  2179.0 35.8 convolution_convert_fusion.1
  2214.9 36.6 copy.190
  2284.4 40.4 %fusion.59 = f32[4,256,128]{2,1,0:T(8,128)S(1)} fusion(f32[4,80,64,128]{3,2,1,0:T(8,128)} %get-tuple-element.486, f32[4,256,80,64]{1,0,3,2:T(4,128)} %reshape.225, f32[4,256,80]{1,2,0:T(8,128)S(1)} %copy-done.16), kind=kOutput, calls=%fused_computation.111 | convolution fusion | flops 8058306560 | bytes 32309248 | tf_op jit(solution)/shard_map/transpose(jvp(bln,bhpn,bhl->blhp))/dot_general | solution.py:77
  2325.9 37.2 convolution_bitcast_fusion
  2382.8 56.5 %multiply_reduce_fusion.4 = (f32[5376]{0:T(1024)S(1)}, f32[5376]{0:T(1024)S(1)}, f32[5376]{0:T(1024)S(1)}, f32[5376]{0:T(1024)}, f32[5376]{0:T(1024)S(1)}, /*index=5*/f32[1024,5376]{1,0:T(8,128)}) fusion(f32[1024,5376]{1,0:T(8,128)} %slice.71, f32[1024,10496]{1,0:T(8,128)} %fusion.87, f32[1024,5376]{1,0:T(8,128)} %get-tuple-element.296, ...), kind=kLoop, calls=%fused_computation.48 | loop fusion | flops 110073600 | bytes 110208000 | tf_op jit(solution)/shard_map/transpose(jvp())/reduce_sum | solution.py:88
  2473.9 36.2 pad_add_fusion
  2510.1 71.6 %convolution_convert_fusion = bf16[2560,10496]{1,0:T(8,128)(2,1)} fusion(f32[1024,5120]{1,0:T(8,128)} %get-tuple-element.300, f32[1024,5376]{1,0:T(8,128)} %pad_add_fusion, bf16[1024,2560]{1,0:T(8,128)(2,1)} %param.16, f32[2560]{0:T(1024)S(1)} %copy-done.60, f32[1024]{0:T(1024)S(1)} %copy-done.66), kind=kOutput, calls=%fused_computation.21 | convolution fusion | flops 55088119808 | bytes 101988352 | tf_op jit(solution)/shard_map/dot_general | solution.py:41
  2584.1 449.7 %reduce-scatter.6.cloned.1.call-done = bf16[640,10496]{1,0:T(8,128)(2,1)} async-done(((bf16[2560,10496]{1,0:T(8,128)(2,1)}), bf16[640,10496]{1,0:T(8,128)(2,1)}) %reduce-scatter.6.cloned.1.call-update) | async-done | bytes 13434896 | tf_op jit(solution)/shard_map/reduce_scatter | solution.py:143
  3036.0 41.4 %fusion.48 = bf16[1024,2560]{1,0:T(8,128)(2,1)} fusion(bf16[1024,2560]{1,0:T(8,128)(2,1)} %param.16, bf16[5120,2560]{1,0:T(8,128)(2,1)} %all-gather.3.cloned.1.call-done, f32[1024,5120]{1,0:T(8,128)} %get-tuple-element.294, f32[5120]{0:T(1024)S(1)} %copy-done.71, f32[1024]{0:T(1024)S(1)} %copy-done.75), kind=kOutput, calls=%fused_computation.100 | convolution fusion | flops 26867138560 | bytes 57696256 | tf_op jit(solution)/shard_map/dot_general | solution.py:126
  3077.4 424.6 %all-gather.5.cloned.1.call-done = bf16[2560,10496]{1,0:T(8,128)(2,1)} async-done(((bf16[640,10496]{1,0:T(8,128)(2,1)}), bf16[2560,10496]{1,0:T(8,128)(2,1)}) %all-gather.5.cloned.1.call-update) | async-done | bytes 53739536 | tf_op jit(solution)/shard_map/all_gather | solution.py:162
  3502.0 72.3 %fusion.58 = f32[1024,2560]{1,0:T(8,128)} fusion(bf16[2560,10496]{1,0:T(8,128)(2,1)} %all-gather.5.cloned.1.call-done, f32[1024,5120]{1,0:T(8,128)} %get-tuple-element.300, f32[1024,5376]{1,0:T(8,128)} %pad_add_fusion), kind=kOutput, calls=%fused_computation.108 | convolution fusion | flops 55050764288 | bytes 107216896 | tf_op jit(solution)/shard_map/dot_general | solution.py:47
  3589.6 41.6 %all-reduce.16 = (f32[2560]{0:T(1024)}, f32[5376]{0:T(1024)}, f32[80]{0:T(128)}, f32[80]{0:T(128)}, f32[80]{0:T(128)}, /*index=5*/f32[5120]{0:T(1024)}) all-reduce(f32[2560]{0:T(1024)S(1)} %get-tuple-element.247, f32[5376]{0:T(1024)S(1)} %copy-done.51, ...), channel_id=1, replica_groups=mesh['replica'=8,'shard'=4] {'replica','shard'}, use_global_device_ids=true, to_apply=%region_25.26 | all-reduce | flops 13296 | bytes 106368 | tf_op jit(solution)/shard_map/psum | solution.py:168
  3631.1 272.8 %all-reduce.23.cloned.1.call-done = (bf16[640,10496]{1,0:T(8,128)(2,1)}, bf16[640,80]{0,1:T(8,128)(2,1)}, bf16[1280,2560]{1,0:T(8,128)(2,1)}) async-done(((bf16[640,10496]{1,0:T(8,128)(2,1)}, bf16[640,80]{0,1:T(8,128)(2,1)}, bf16[1280,2560]{1,0:T(8,128)(2,1)}), (bf16[640,10496]{1,0:T(8,128)(2,1)}, bf16[640,80]{0,1:T(8,128)(2,1)}, bf16[1280,2560]{1,0:T(8,128)(2,1)})) %all-reduce.23.cloned.1.call-update) | async-done | bytes 20090896 | tf_op jit(solution)/shard_map/psum | solution.py:157
  3927.5 105.0 %all-reduce.21.cloned.1.call-done = f32[4,5376]{1,0:T(4,128)} async-done(((f32[4,5376]{1,0:T(4,128)}), f32[4,5376]{1,0:T(4,128)}) %all-reduce.21.cloned.1.call-update) | async-done | bytes 86032 | tf_op jit(solution)/shard_map/psum | solution.py:168
  (344 shorter events, 723.9 us)
Async XLA Ops:
  7.2 1097.4 %copy-start.83 = (f32[80]{0:T(128)S(1)}, f32[80]{0:T(128)}, u32[]{:S(2)}) copy-start(f32[80]{0:T(128)} %param.25) | copy-start | bytes 964
  7.2 1098.8 %copy-start.52 = (f32[4,5376]{1,0:T(4,128)S(1)}, f32[4,5376]{1,0:T(4,128)}, u32[]{:S(2)}) copy-start(f32[4,5376]{1,0:T(4,128)} %param.21) | copy-start | bytes 258052
  7.2 1654.4 %all-gather.3.cloned.1.call-start = ((), (), s32[]{:S(2)}) async-start(), calls=%async_computation.3 | async-start | bytes 32768000 | tf_op jit(solution)/shard_map/all_gather | solution.py:128
  7.2 292.7 %collective-permute-start = (bf16[640,10496]{1,0:T(8,128)(2,1)}, bf16[640,10496]{1,0:T(8,128)(2,1)}, u32[]{:S(2)}, u32[]{:S(2)}) collective-permute-start(bf16[640,10496]{1,0:T(8,128)(2,1)} %param.17), channel_id=1, source_target_pairs={{0,1},{1,2},{2,3},{3,0},{4,5},{5,6},{6,7},{7,4},{8,9},{9,10},{10,1... | collective-permute-start | bytes 40304648 | tf_op jit(solution)/shard_map/ppermute | solution.py:24
  8.8 1137.3 %collective-permute-start.1 = (bf16[640,10496]{1,0:T(8,128)(2,1)}, bf16[640,10496]{1,0:T(8,128)(2,1)}, u32[]{:S(2)}, u32[]{:S(2)}) collective-permute-start(bf16[640,10496]{1,0:T(8,128)(2,1)} %param.17), channel_id=1, source_target_pairs={{0,3},{1,0},{2,1},{3,2},{4,7},{5,4},{6,5},{7,6},{8,11},{9,8},{10,9... | collective-permute-start | bytes 40304648 | tf_op jit(solution)/shard_map/ppermute | solution.py:29
  300.0 859.0 %collective-permute-start.2 = (bf16[640,10496]{1,0:T(8,128)(2,1)}, bf16[640,10496]{1,0:T(8,128)(2,1)}, u32[]{:S(2)}, u32[]{:S(2)}) collective-permute-start(bf16[640,10496]{1,0:T(8,128)(2,1)} %collective-permute-done), channel_id=1, source_target_pairs={{0,1},{1,2},{2,3},{3,0},{4,5},{5,6},{6,7},{7,4},{8,9},{9,10},{10,1... | collective-permute-start | bytes 40304648 | tf_op jit(solution)/shard_map/ppermute | solution.py:24
  300.6 2281.8 %reduce-scatter.10.cloned.1.call-start = ((), (), s32[]{:S(2)}) async-start(), calls=%async_computation.8 | async-start | bytes 819200
  1960.2 81.8 %copy-start.4 = (f32[80,64,128]{2,1,0:T(8,128)S(1)}, f32[80,64,128]{2,1,0:T(8,128)}, u32[]{:S(2)}) copy-start(f32[80,64,128]{2,1,0:T(8,128)} %custom-call.1) | copy-start | bytes 7864324
  2178.9 405.2 %reduce-scatter.8.cloned.1.call-start = ((), (), s32[]{:S(2)}) async-start(), calls=%async_computation.6 | async-start | bytes 32768000 | tf_op jit(solution)/shard_map/reduce_scatter | solution.py:132
  2214.8 819.0 %reduce-scatter.6.cloned.1.call-start = ((), (), s32[]{:S(2)}) async-start(), calls=%async_computation.5 | async-start | bytes 67174400 | tf_op jit(solution)/shard_map/reduce_scatter | solution.py:143
  2284.3 80.7 %slice-start = ((s8[20971520]{0:T(1024)(128)(4,1)}), s8[4194304]{0:T(1024)(128)(4,1)S(1)}, s32[]{:S(2)}) async-start(s8[20971520]{0:T(1024)(128)(4,1)} %bitcast.192), calls=%async_computation.10 | async-start | bytes 8388608
  2284.4 80.7 %slice-start.1 = ((s8[20971520]{0:T(1024)(128)(4,1)}), s8[4194304]{0:T(1024)(128)(4,1)S(1)}, s32[]{:S(2)}) async-start(s8[20971520]{0:T(1024)(128)(4,1)} %bitcast.192), calls=%async_computation.11 | async-start | bytes 8388608
  2581.7 452.3 %copy-start.53 = (f32[5120]{0:T(1024)S(1)}, f32[5120]{0:T(1024)}, u32[]{:S(2)}) copy-start(f32[5120]{0:T(1024)} %get-tuple-element.288) | copy-start | bytes 61444
  2581.7 453.0 %copy-start.81 = (f32[80]{0:T(128)S(1)}, f32[80]{0:T(128)}, u32[]{:S(2)}) copy-start(f32[80]{0:T(128)} %get-tuple-element.309) | copy-start | bytes 964
  2581.7 453.0 %copy-start.84 = (f32[80]{0:T(128)S(1)}, f32[80]{0:T(128)}, u32[]{:S(2)}) copy-start(f32[80]{0:T(128)} %param.24) | copy-start | bytes 964
  2581.7 454.2 %copy-start.71 = (f32[5120]{0:T(1024)S(1)}, f32[5120]{0:T(1024)}, u32[]{:S(2)}) copy-start(f32[5120]{0:T(1024)} %param.26) | copy-start | bytes 61444
  2581.7 454.2 %copy-start.75 = (f32[1024]{0:T(1024)S(1)}, f32[1024]{0:T(1024)}, u32[]{:S(2)}) copy-start(f32[1024]{0:T(1024)} %copy-done.73) | copy-start | bytes 12292
  2581.7 920.3 %all-gather.5.cloned.1.call-start = ((), (), s32[]{:S(2)}) async-start(), calls=%async_computation.4 | async-start | bytes 67174400 | tf_op jit(solution)/shard_map/all_gather | solution.py:162
  2582.3 1321.6 %all-reduce.23.cloned.1.call-start = ((), (), s32[]{:S(2)}) async-start(), calls=%async_computation.9 | async-start | bytes 40181760 | tf_op jit(solution)/shard_map/psum | solution.py:157
  3033.8 998.7 %all-reduce.21.cloned.1.call-start = ((), (), s32[]{:S(2)}) async-start(), calls=%async_computation.7 | async-start | bytes 172032 | tf_op jit(solution)/shard_map/psum | solution.py:168
  3077.4 496.9 %copy-start.24 = (bf16[2560,80]{0,1:T(8,128)(2,1)S(1)}, bf16[2560,80]{0,1:T(8,128)(2,1)}, u32[]{:S(2)}) copy-start(bf16[2560,80]{0,1:T(8,128)(2,1)} %copy-done.23) | copy-start | bytes 1228804
  3077.4 496.9 %copy-start.31 = (bf16[1024,80]{0,1:T(8,128)(2,1)S(1)}, bf16[1024,80]{0,1:T(8,128)(2,1)}, u32[]{:S(2)}) copy-start(bf16[1024,80]{0,1:T(8,128)(2,1)} %copy-done.30) | copy-start | bytes 491524
  3077.4 496.9 %copy-start.61 = (f32[2560]{0:T(1024)S(1)}, f32[2560]{0:T(1024)}, u32[]{:S(2)}) copy-start(f32[2560]{0:T(1024)} %param.20) | copy-start | bytes 30724
  3077.4 496.9 %copy-start.67 = (f32[1024]{0:T(1024)S(1)}, f32[1024]{0:T(1024)}, u32[]{:S(2)}) copy-start(f32[1024]{0:T(1024)} %copy-done.64) | copy-start | bytes 12292
  (84 other events, 2390.5 us)
Sparse Core Ops, SparseCore 0:
  300.7 647.5 all-gather.2
  2179.0 25.7 reduce-scatter.9
  2215.0 230.6 reduce-scatter.7
  2581.8 451.9 reduce-scatter.5
  3035.7 466.2 all-gather.4
  3505.5 398.3 all-reduce.22
  3910.1 122.3 all-reduce.20
